TPU v7x, 256 devices: a whole 4x4x8 slice. The times are simulated.
256 devices in a mesh: blk: 16 (over z, x_hi), leaf: 8 (over y, core), rhs: 2 (over x_lo).
Axes of the slice: x: 4 (x_hi: 2, x_lo: 2; x = x_hi * 2 + x_lo), y: 4, z: 8, core: 2. Of those that a mesh axis runs over, the one named last changes fastest.
Arguments:
- residual: float32 [32, 8, 65536], P('rhs', 'leaf', 'blk'), may hold values from -160 to 160
- points: float32 [3, 8, 65536], P(None, 'leaf', 'blk'), may hold values from -12330 to 12330
- noise: float32 [8, 65536], P('leaf', 'blk'), may hold values from 1 to 2
- block_list: int32 [8, 8, 256], P('leaf'), may hold values from 0 to 1, as said below
Outputs:
- correction: float32 [32, 8, 65536], P('rhs', 'leaf', 'blk')
- new_residual: float32 [32, 8, 65536], P('rhs', 'leaf', 'blk')
- basis: float32 [128, 8, 65536], P('rhs', 'leaf', 'blk')
Inputs may be any that keep to these rules, and one draw needn't show every extreme that they name: The list is symmetric: block_list[t, k, i] == block_list[t, 7 - k, (i + d) mod 256] with d the offset of entry k.
All inputs are finite; a program needn't handle non-finite values.
Results may differ from a plain program's by a relative error of at most 0.007.
Values sent between devices are 32-bit elements; how exact they have to be, the bound alone decides.
A program may use at most 128 MiB of HBM per device.

v0:
```python
import jax
import jax.numpy as jnp
from jax import lax
from jax.sharding import PartitionSpec as P

M = 32
S = 4
BS = 256
REACH = 4
SUPPORT = 1408
centre_shift = 1.5
amplitude = 1.1
exact = lax.Precision.HIGHEST


def extended(x, sides, width):
    for axis, dim in sides:
        count, length = (lax.axis_size(axis), x.shape[dim])
        up = [(i, (i + 1) % count) for i in range(count)]
        down = [(j, i) for i, j in up]
        last = lax.slice_in_dim(x, length - width, length, axis=dim)
        leading = lax.slice_in_dim(x, 0, width, axis=dim)
        before = lax.ppermute(last, axis, up)
        after = lax.ppermute(leading, axis, down)
        x = jnp.concatenate([before, x, after], axis=dim)
    return x


def kernel_tile(near_points, own_points):
    squared = (near_points[0][:, None] - own_points[0][None, :]) ** 2
    squared = squared + (near_points[1][:, None] - own_points[1][None, :]) ** 2
    squared = squared + (near_points[2][:, None] - own_points[2][None, :]) ** 2
    radius = jnp.sqrt(squared) / SUPPORT
    remain = jnp.maximum(1.0 - radius, 0.0)
    return remain * remain * (remain * remain) * (4.0 * radius + 1.0) * (amplitude / SUPPORT)


def band_product(field_wide, points_wide, weights, rows_out):
    per_turn = rows_out // 8
    count = field_wide.shape[0]

    def turn(carry, index):
        pieces = []
        for inner in range(per_turn):
            block = index * per_turn + inner
            own_points = lax.dynamic_slice_in_dim(points_wide, (block + REACH) * BS, BS, 1)
            total = jnp.zeros((count, BS), jnp.float32)
            for offset in range(2 * REACH + 1):
                column_at = (block + offset) * BS
                near_points = lax.dynamic_slice_in_dim(points_wide, column_at, BS, 1)
                near_field = lax.dynamic_slice_in_dim(field_wide, column_at, BS, 1)
                listed = lax.dynamic_index_in_dim(weights[offset], block, 0, False)
                tile = kernel_tile(near_points, own_points) * listed
                total = total + jnp.dot(near_field, tile, precision=exact)
            pieces.append(total)
        return (carry, jnp.concatenate(pieces, axis=1))

    carry, parts = lax.scan(turn, jnp.zeros((), jnp.int32), jnp.arange(8, dtype=jnp.int32))
    return jnp.moveaxis(parts, 0, 1).reshape(count, rows_out * BS)


def galerkin(gram, count_points, count_sides):
    normed = gram / count_points
    basis_count = normed.shape[0] - count_sides
    gram_basis = normed[:basis_count, :basis_count]
    factor_low = jnp.linalg.cholesky(gram_basis)
    inverse_low = lax.linalg.triangular_solve(
        factor_low, jnp.eye(basis_count, dtype=jnp.float32), left_side=True, lower=True
    )
    cross = normed[:basis_count, count_sides:] + centre_shift * gram_basis
    projected = jnp.dot(
        jnp.dot(inverse_low, cross, precision=exact), inverse_low.T, precision=exact
    )
    projected = 0.5 * (projected + projected.T)
    small_side = jnp.dot(inverse_low, gram_basis[:, :count_sides], precision=exact)
    proj_factor = jnp.linalg.cholesky(projected)
    halfway = lax.linalg.triangular_solve(proj_factor, small_side, left_side=True, lower=True)
    coeffs = lax.linalg.triangular_solve(
        proj_factor, halfway, left_side=True, lower=True, transpose_a=True
    )
    combo = jnp.dot(coeffs.T, inverse_low, precision=exact)
    return (inverse_low, combo)


def row_products(rows):
    return lax.dot_general(rows, rows, (((1,), (1,)), ((), ())), precision=exact)


def local(residual, points, noise, block_list):
    field = residual[:, 0]
    coords = points[:, 0]
    nugget = noise[0]
    own_rows = field.shape[1]
    own_blocks = own_rows // BS
    first_block = lax.axis_index("blk") * own_blocks
    listed = block_list[0].astype(jnp.float32)
    nine = jnp.concatenate(
        [listed[:REACH], jnp.ones((1, listed.shape[1]), jnp.float32), listed[REACH:]], axis=0
    )
    margin = S * REACH
    wrapped = jnp.concatenate([nine[:, -margin:], nine, nine[:, :margin]], axis=1)
    powers = [field]
    rim = REACH * BS
    coords_wide = extended(coords, (("blk", 1),), rim)
    own_weights = lax.dynamic_slice_in_dim(wrapped, first_block + margin, own_blocks, 1)
    current = field
    for power_step in range(S):
        widened = extended(current, (("blk", 1),), rim)
        current = (
            band_product(widened, coords_wide, own_weights, own_blocks)
            + (nugget - centre_shift) * current
        )
        powers.append(current)
    half_panel = jnp.stack(powers, axis=0)
    count_points = own_rows * lax.axis_size("blk") * lax.axis_size("leaf")
    sides_here = field.shape[0]
    whole = lax.all_gather(half_panel, "rhs", axis=1, tiled=True)
    flat = whole.reshape(-1, own_rows)
    gram = lax.psum(row_products(flat), ("blk", "leaf"))
    inverse_low, combo = galerkin(gram, count_points, M)
    first_rows = flat[: S * M]
    image = flat[M:] + centre_shift * first_rows
    part = lax.axis_index("rhs")
    basis_here = S * M // lax.axis_size("rhs")
    mine_low = lax.dynamic_slice_in_dim(inverse_low, part * basis_here, basis_here, 0)
    mine_combo = lax.dynamic_slice_in_dim(combo, part * sides_here, sides_here, 0)
    correction = jnp.dot(mine_combo, first_rows, precision=exact)
    new_residual = field - jnp.dot(mine_combo, image, precision=exact)
    basis = jnp.dot(mine_low, first_rows, precision=exact)
    return (correction[:, None], new_residual[:, None], basis[:, None])


def solution(mesh):
    placed = (
        P("rhs", "leaf", "blk"),
        P(None, "leaf", "blk"),
        P("leaf", "blk"),
        P("leaf", None, None),
    )
    return jax.shard_map(
        local,
        mesh=mesh,
        in_specs=placed,
        out_specs=(P("rhs", "leaf", "blk"), P("rhs", "leaf", "blk"), P("rhs", "leaf", "blk")),
        check_vma=False,
    )
```

profile of v0, /device:TPU:2, one launch (start us, length us, event | category | flops | bytes accessed | tf_op | source)
XLA Modules:
  0.0 2114.2 jit_solution(17787421845742051918)
XLA Ops:
  7.2 0.8 copy.48
  8.1 2.2 collective-permute-start.2
  10.3 5.4 collective-permute-start.3
  15.6 1.1 copy.47
  16.9 5.6 collective-permute-start.1
  22.5 1.1 bitcast_dynamic-update-slice_fusion
  23.6 0.7 convert_element_type.5
  24.4 0.7 broadcast_add_fusion
  25.4 206.0 %while.52 = (s32[]{:T(128)}, f32[8,16,512]{2,1,0:T(8,128)S(1)}, s32[8]{0:T(128)S(1)}, f32[16,6144]{1,0:T(8,128)S(1)}, f32[3,6144]{1,0:T(4,128)S(1)}, /*index=5*/...) while((s32[]{:T(128)}, f32[8,16,512]{2,1,0:T(8,128)S(1)}, ...), condition=%wide.region_1.2_spmd, body=%wide.region_0.1_spmd.sunk | while | flops 246620224 | bytes 1092197 | solution.py:58
  38.6 0.7 constant_dynamic-slice_fusion.141
  64.3 0.7 constant_dynamic-slice_fusion.141
  167.3 0.7 constant_dynamic-slice_fusion.141
  193.0 0.7 constant_dynamic-slice_fusion.141
  231.9 5.6 collective-permute-start.5
  237.9 1.8 collective-permute-done.4
  239.8 202.8 %while.53 = (s32[]{:T(128)}, f32[8,16,512]{2,1,0:T(8,128)S(1)}, s32[8]{0:T(128)S(1)}, f32[16,6144]{1,0:T(8,128)S(1)}, f32[3,6144]{1,0:T(4,128)S(1)}, /*index=5*/...) while((s32[]{:T(128)}, f32[8,16,512]{2,1,0:T(8,128)S(1)}, ...), condition=%wide.region_3.4_spmd, body=%wide.region_2.3_spmd.sunk | while | flops 246620224 | bytes 1092197 | solution.py:58
  442.8 6.1 collective-permute-start.7
  449.2 1.5 collective-permute-done.6
  450.9 203.8 %while.54 = (s32[]{:T(128)}, f32[8,16,512]{2,1,0:T(8,128)S(1)}, s32[8]{0:T(128)S(1)}, f32[16,6144]{1,0:T(8,128)S(1)}, f32[3,6144]{1,0:T(4,128)S(1)}, /*index=5*/...) while((s32[]{:T(128)}, f32[8,16,512]{2,1,0:T(8,128)S(1)}, ...), condition=%wide.region_5.6_spmd, body=%wide.region_4.5_spmd.sunk | while | flops 246620224 | bytes 1092197 | solution.py:58
  654.8 1.9 collective-permute-start.8
  656.7 4.4 collective-permute-start.9
  661.4 1.8 collective-permute-done.8
  663.4 207.7 %while.55 = (s32[]{:T(128)}, f32[8,16,512]{2,1,0:T(8,128)S(1)}, s32[8]{0:T(128)S(1)}, f32[16,6144]{1,0:T(8,128)S(1)}, f32[3,6144]{1,0:T(4,128)S(1)}, /*index=5*/...) while((s32[]{:T(128)}, f32[8,16,512]{2,1,0:T(8,128)S(1)}, ...), condition=%wide.region_7.8_spmd, body=%wide.region_6.7_spmd.sunk | while | flops 246620224 | bytes 1092197 | solution.py:58
  676.8 0.7 constant_dynamic-slice_fusion.159
  702.7 0.7 constant_dynamic-slice_fusion.159
  728.7 0.7 constant_dynamic-slice_fusion.159
  754.7 0.7 constant_dynamic-slice_fusion.159
  780.6 0.7 constant_dynamic-slice_fusion.159
  806.6 0.7 constant_dynamic-slice_fusion.159
  832.5 0.7 constant_dynamic-slice_fusion.159
  858.5 0.7 constant_dynamic-slice_fusion.159
  871.3 1.0 copy-done.4
  872.7 45.1 %all-gather.2.cloned.1.call-done = f32[5,32,4096]{2,1,0:T(8,128)} async-done(((f32[5,16,4096]{2,1,0:T(8,128)}), f32[5,32,4096]{2,1,0:T(8,128)}) %all-gather.2.cloned.1.call-update) | async-done | bytes 2621456 | tf_op jit(solution)/shard_map/all_gather | solution.py:117
  917.8 5.6 fusion.2577
  923.9 1.3 copy-done.1
  925.2 1.6 bitcast_add_fusion
  926.8 1122.0 %all-reduce.2.cloned.1.call-done = f32[160,160]{0,1:T(8,128)} async-done(((f32[160,160]{0,1:T(8,128)}), f32[160,160]{0,1:T(8,128)}) %all-reduce.2.cloned.1.call-update) | async-done | bytes 102416 | tf_op jit(solution)/shard_map/psum | solution.py:119
  2048.8 0.9 broadcast_multiply_fusion
  2049.9 11.7 cholesky.44
  2062.9 9.8 custom-call.10
  2074.0 12.0 cholesky.55
  2087.3 9.8 custom-call.11
  2097.8 2.7 fusion.2532
  2100.6 1.0 copy.29
  2101.6 1.1 convolution_bitcast_fusion.1
  2102.7 1.2 convolution_bitcast_fusion
  2103.9 2.0 copy.30
  2105.9 1.0 copy.28
  (936 shorter events, 413.4 us)
Async XLA Ops:
  7.2 910.6 %all-gather.2.cloned.1.call-start = ((), (), s32[]{:S(2)}) async-start(), calls=%async_computation | async-start | bytes 3932160 | tf_op jit(solution)/shard_map/all_gather | solution.py:117
  8.1 17.2 collective-permute-start.2
  10.3 15.0 collective-permute-start.3
  16.8 8.5 collective-permute-start
  16.9 8.4 collective-permute-start.1
  25.4 206.0 %copy-start.3 = (f32[16,1,4096]{2,1,0:T(1,128)S(1)}, f32[16,1,4096]{2,1,0:T(1,128)}, u32[]{:S(2)}) copy-start(f32[16,1,4096]{2,1,0:T(1,128)} %param.13) | copy-start | bytes 786436
  231.6 8.2 collective-permute-start.4
  231.9 7.9 collective-permute-start.5
  442.7 8.0 collective-permute-start.6
  442.8 8.0 collective-permute-start.7
  654.8 8.4 collective-permute-start.8
  656.7 6.6 collective-permute-start.9
  871.3 1.1 copy-start.4
  872.4 1176.4 %all-reduce.2.cloned.1.call-start = ((), (), s32[]{:S(2)}) async-start(), calls=%async_computation.1 | async-start | bytes 327680 | tf_op jit(solution)/shard_map/psum | solution.py:119
  917.8 5.6 copy-start
  923.9 1.3 copy-start.1
  2073.9 27.7 %copy-start.2 = (f32[4,32,4096]{2,1,0:T(8,128)S(1)}, f32[4,32,4096]{2,1,0:T(8,128)}, u32[]{:S(2)}) copy-start(f32[4,32,4096]{2,1,0:T(8,128)} %copy-done.1) | copy-start | bytes 6291460
Sparse Core Ops, SparseCore 0:
  872.5 45.1 all-gather.1
  923.5 1125.2 all-reduce.1
where the time goes:
time: 2130 us; the launch traced here: 2110 us
  waiting for transfers between devices  1170 us (55%)
  loops' own time  407 us (19%)
  matrix products  296 us (14%)
  local copies, waits for them, and re-layouts  140 us (7%)
  other arithmetic  51.7 us (2%)
  starting transfers between devices  32 us (2%)
    psum x1, waiting for transfers between devices, local(): gram = lax.psum(row_products(flat), ('blk', 'leaf'))  1120 us
    another operation x4, loops' own time, band_product(): lax.scan(turn, jnp.zeros((), jnp.int32), jnp.arange(8, dtype=jnp.int32))  407 us
    dot_general x576, matrix products, turn(): total = total + jnp.dot(near_field, tile, precision=exact)  284 us
    dynamic_slice x160, local copies, waits for them, and re-layouts, turn(): listed = lax.dynamic_index_in_dim(weights[offset], block, 0, False)  105 us
    all_gather x1, waiting for transfers between devices, local(): whole = lax.all_gather(half_panel, 'rhs', axis=1, tiled=True)  45.1 us
  transfers between devices with their start and end apart: 12, of which 7 were waited for; matrix products, arithmetic and copies ran while one was open for 0% of the time, Pallas kernels for 0%

commit v1 on v0

--- a/solution.py
+++ b/solution.py
@@ -116,7 +116,7 @@
     sides_here = field.shape[0]
     whole = lax.all_gather(half_panel, "rhs", axis=1, tiled=True)
     flat = whole.reshape(-1, own_rows)
-    gram = lax.psum(row_products(flat), ("blk", "leaf"))
+    gram = jnp.sum(lax.all_gather(row_products(flat), ("blk", "leaf")), axis=0)
     inverse_low, combo = galerkin(gram, count_points, M)
     first_rows = flat[: S * M]
     image = flat[M:] + centre_shift * first_rows

time: 2130 us -> 1190 us (0.56)
  waiting for transfers between devices: 1170 us -> 215 us
  loops' own time: 407 us -> 429 us
    psum x1 -> x0, waiting for transfers between devices: 1120 us -> none  [local(): gram = lax.psum(row_products(flat), ('blk', 'leaf'))]
    all_gather x0 -> x1, waiting for transfers between devices: none -> 164 us  [local(): gram = jnp.sum(lax.all_gather(row_products(flat), ('blk', 'leaf')), axis=0)]
    another operation x4, loops' own time: 407 us -> 429 us  [band_product(): lax.scan(turn, jnp.zeros((), jnp.int32), jnp.arange(8, dtype=jnp.int32))]
  transfers between devices with their start and end apart: 12 -> 12, of which waited for: 7 -> 7; matrix products, arithmetic and copies ran while one was open for 0% -> 1% of each run, Pallas kernels for 0% -> 0%
where the time goes in v1:
time: 1190 us; the launch traced here: 1180 us
  loops' own time  429 us (36%)
  matrix products  282 us (24%)
  waiting for transfers between devices  215 us (18%)
  local copies, waits for them, and re-layouts  143 us (12%)
  other arithmetic  59.3 us (5%)
  starting transfers between devices  31.8 us (3%)
  between operations  15 us (1%)
    another operation x4, loops' own time, band_product(): lax.scan(turn, jnp.zeros((), jnp.int32), jnp.arange(8, dtype=jnp.int32))  429 us
    dot_general x576, matrix products, turn(): total = total + jnp.dot(near_field, tile, precision=exact)  272 us
    all_gather x1, waiting for transfers between devices, local(): gram = jnp.sum(lax.all_gather(row_products(flat), ('blk', 'leaf')), axis=0)  164 us
    dynamic_slice x160, local copies, waits for them, and re-layouts, turn(): listed = lax.dynamic_index_in_dim(weights[offset], block, 0, False)  107 us
    all_gather x1, waiting for transfers between devices, local(): whole = lax.all_gather(half_panel, 'rhs', axis=1, tiled=True)  45.3 us
    ppermute x5, starting transfers between devices, extended(): after = lax.ppermute(leading, axis, down)  27.2 us
  transfers between devices with their start and end apart: 12, of which 7 were waited for; matrix products, arithmetic and copies ran while one was open for 1% of the time, Pallas kernels for 0%

profile of v1, /device:TPU:2, one launch (start us, length us, event | category | flops | bytes accessed | tf_op | source)
XLA Modules:
  0.0 1175.2 jit_solution(12501122035800270083)
XLA Ops:
  7.2 0.8 copy.59
  8.1 2.2 collective-permute-start.2
  10.3 5.4 collective-permute-start.3
  15.6 1.1 copy.58
  16.9 5.6 collective-permute-start.1
  22.5 1.1 bitcast_dynamic-update-slice_fusion
  23.6 0.7 convert_element_type.5
  24.4 0.7 broadcast_add_fusion
  25.4 208.2 %while.52 = (s32[]{:T(128)}, f32[8,16,512]{2,1,0:T(8,128)S(1)}, s32[8]{0:T(128)S(1)}, f32[16,6144]{1,0:T(8,128)S(1)}, f32[3,6144]{1,0:T(4,128)S(1)}, /*index=5*/...) while((s32[]{:T(128)}, f32[8,16,512]{2,1,0:T(8,128)S(1)}, ...), condition=%wide.region_1.2_spmd, body=%wide.region_0.1_spmd.sunk | while | flops 246620224 | bytes 1092189 | solution.py:58
  38.1 0.7 constant_dynamic-slice_fusion.141
  90.2 0.7 constant_dynamic-slice_fusion.141
  116.2 0.7 constant_dynamic-slice_fusion.141
  142.2 0.7 constant_dynamic-slice_fusion.141
  234.1 5.6 collective-permute-start.5
  240.1 1.8 collective-permute-done.4
  242.1 208.9 %while.53 = (s32[]{:T(128)}, f32[8,16,512]{2,1,0:T(8,128)S(1)}, s32[8]{0:T(128)S(1)}, f32[16,6144]{1,0:T(8,128)S(1)}, f32[3,6144]{1,0:T(4,128)S(1)}, /*index=5*/...) while((s32[]{:T(128)}, f32[8,16,512]{2,1,0:T(8,128)S(1)}, ...), condition=%wide.region_3.4_spmd, body=%wide.region_2.3_spmd.sunk | while | flops 246620224 | bytes 1092189 | solution.py:58
  451.2 6.1 collective-permute-start.7
  457.5 1.5 collective-permute-done.6
  459.3 207.4 %while.54 = (s32[]{:T(128)}, f32[8,16,512]{2,1,0:T(8,128)S(1)}, s32[8]{0:T(128)S(1)}, f32[16,6144]{1,0:T(8,128)S(1)}, f32[3,6144]{1,0:T(4,128)S(1)}, /*index=5*/...) while((s32[]{:T(128)}, f32[8,16,512]{2,1,0:T(8,128)S(1)}, ...), condition=%wide.region_5.6_spmd, body=%wide.region_4.5_spmd.sunk | while | flops 246620224 | bytes 1092189 | solution.py:58
  666.8 1.9 collective-permute-start.8
  668.7 4.4 collective-permute-start.9
  673.4 1.8 collective-permute-done.8
  675.4 208.7 %while.55 = (s32[]{:T(128)}, f32[8,16,512]{2,1,0:T(8,128)S(1)}, s32[8]{0:T(128)S(1)}, f32[16,6144]{1,0:T(8,128)S(1)}, f32[3,6144]{1,0:T(4,128)S(1)}, /*index=5*/...) while((s32[]{:T(128)}, f32[8,16,512]{2,1,0:T(8,128)S(1)}, ...), condition=%wide.region_7.8_spmd, body=%wide.region_6.7_spmd.sunk | while | flops 246620224 | bytes 1092189 | solution.py:58
  679.2 0.7 constant_dynamic-slice_fusion.156
  705.3 0.7 constant_dynamic-slice_fusion.156
  731.4 0.7 constant_dynamic-slice_fusion.156
  757.5 0.7 constant_dynamic-slice_fusion.156
  783.6 0.7 constant_dynamic-slice_fusion.156
  809.7 0.7 constant_dynamic-slice_fusion.156
  835.7 0.7 constant_dynamic-slice_fusion.156
  861.8 0.7 constant_dynamic-slice_fusion.156
  884.4 1.1 copy-done.5
  885.5 45.3 %all-gather.4.cloned.1.call-done = f32[5,32,4096]{2,1,0:T(8,128)} async-done(((f32[5,16,4096]{2,1,0:T(8,128)}), f32[5,32,4096]{2,1,0:T(8,128)}) %all-gather.4.cloned.1.call-update) | async-done | bytes 2621456 | tf_op jit(solution)/shard_map/all_gather | solution.py:117
  930.8 5.6 fusion.2577
  937.0 1.4 copy-done.1
  938.3 1.6 bitcast_add_fusion
  939.9 164.0 %all-gather.6.cloned.1.call-done = f32[20480,160]{1,0:T(8,128)} async-done(((f32[160,160]{1,0:T(8,128)}), f32[20480,160]{1,0:T(8,128)}) %all-gather.6.cloned.1.call-update) | async-done | bytes 13107216 | tf_op jit(solution)/shard_map/all_gather | solution.py:119
  1103.9 8.5 reduce_sum.9
  1112.6 11.7 cholesky.44
  1125.7 9.8 custom-call.10
  1136.3 1.2 convolution_bitcast_fusion
  1137.5 2.0 copy.42
  1140.1 11.9 %cholesky.55 = f32[128,128]{1,0:T(8,128)S(1)} custom-call(f32[128,128]{1,0:T(8,128)S(1)} %fusion.2542), custom_call_target="Cholesky" | custom-call | tf_op jit(solution)/shard_map/jit(cholesky)/cholesky | solution.py:76
  1153.3 9.8 custom-call.11
  1163.7 1.1 convolution_bitcast_fusion.1
  1164.9 1.1 fusion.2532
  1166.0 1.0 copy.41
  1167.0 1.0 copy.40
  (940 shorter events, 403.9 us)
Async XLA Ops:
  7.2 923.7 %all-gather.4.cloned.1.call-start = ((), (), s32[]{:S(2)}) async-start(), calls=%async_computation | async-start | bytes 3932160 | tf_op jit(solution)/shard_map/all_gather | solution.py:117
  8.1 17.2 %collective-permute-start.2 = (f32[3,1024]{1,0:T(4,128)S(1)}, f32[3,1024]{1,0:T(4,128)S(1)}, u32[]{:S(2)}, u32[]{:S(2)}) collective-permute-start(f32[3,1024]{1,0:T(4,128)S(1)} %get-tuple-element.901), channel_id=1, source_target_pairs={{0,16},{16,32},{32,48},{48,64},{64,80},{80,96},{96,112},{112,128},... | collective-permute-start | bytes 36872 | tf_op jit(solution)/shard_map/ppermute | solution.py:23
  10.3 15.0 %collective-permute-start.3 = (f32[3,1024]{1,0:T(4,128)S(1)}, f32[3,1024]{1,0:T(4,128)S(1)}, u32[]{:S(2)}, u32[]{:S(2)}) collective-permute-start(f32[3,1024]{1,0:T(4,128)S(1)} %get-tuple-element.902), channel_id=1, source_target_pairs={{16,0},{32,16},{48,32},{64,48},{80,64},{96,80},{112,96},{128,112},... | collective-permute-start | bytes 36872 | tf_op jit(solution)/shard_map/ppermute | solution.py:24
  16.8 8.5 collective-permute-start
  16.9 8.4 collective-permute-start.1
  25.4 208.2 %copy-start.4 = (f32[16,1,4096]{2,1,0:T(1,128)S(1)}, f32[16,1,4096]{2,1,0:T(1,128)}, u32[]{:S(2)}) copy-start(f32[16,1,4096]{2,1,0:T(1,128)} %param.13) | copy-start | bytes 786436
  233.8 8.2 collective-permute-start.4
  234.1 7.9 collective-permute-start.5
  451.1 8.0 collective-permute-start.6
  451.2 8.0 collective-permute-start.7
  666.8 8.4 collective-permute-start.8
  668.7 6.6 collective-permute-start.9
  884.3 1.1 copy-start.5
  885.5 218.4 %all-gather.6.cloned.1.call-start = ((), (), s32[]{:S(2)}) async-start(), calls=%async_computation.1 | async-start | bytes 21135360 | tf_op jit(solution)/shard_map/all_gather | solution.py:119
  930.8 5.6 copy-start
  937.0 1.4 copy-start.1
  1103.9 32.4 %copy-start.2 = (f32[4,32,4096]{2,1,0:T(8,128)S(1)}, f32[4,32,4096]{2,1,0:T(8,128)}, u32[]{:S(2)}) copy-start(f32[4,32,4096]{2,1,0:T(8,128)} %copy-done.1) | copy-start | bytes 6291460
  1163.2 1.7 copy-start.3
Sparse Core Ops, SparseCore 0:
  885.6 45.1 all-gather.3
  936.6 167.2 all-gather.5
